TPU v7x, 256 devices: a whole 4x4x8 slice. The times are simulated.
256 devices in a mesh: req: 16 (over x, y), seq: 16 (over z, core).
Axes of the slice: x: 4, y: 4, z: 8, core: 2. Of those that a mesh axis runs over, the one named last changes fastest.
Arguments:
- store: bfloat16 [144, 16, 56, 1024], P('req', 'seq'), may hold values from -6 to 6
- passage_owner: int32 [16, 256, 1], P(None, 'seq'), may hold values from 0 to 15; in each aligned block of 16 rows (0 to 15, 16 to 31, ..., all dimensions but the last counted through in order) at most 2 rows name the same one
- passage_slot: int32 [16, 256], P(None, 'seq'), may hold values from 0 to 8
- sel_pos: int32 [16, 1792], P('req'), may hold values from 0 to 14335, as said below
- queries: bfloat16 [16, 1792, 2048], P('req', 'seq'), may hold values from -512 to 512
- new_kv: bfloat16 [16, 1792, 1024], P('req', 'seq'), may hold values from -6 to 6
Outputs:
- blended_kv: bfloat16 [16, 14336, 1024], P('req', 'seq')
- deviation: float32 [16, 1792, 4], P('req', 'seq')
- attended: bfloat16 [16, 1792, 2048], P('req', 'seq')
Inputs may be any that keep to these rules, and one draw needn't show every extreme that they name: `passage_owner`: within the 16 pieces of one request's position block no owner is named more than 2 times, and some block names one owner exactly 2 times. `sel_pos`: entries b * 112 to (b + 1) * 112 - 1 of a request are distinct positions of block b, between b * 896 and (b + 1) * 896 - 1.
All inputs are finite; a program needn't handle non-finite values.
Results may differ from a plain program's by a relative error of at most 0.005.
Values may be sent and summed in bfloat16 or wider, within the bound.
A program may use at most 128 MiB of HBM per device.

v0:
```python
import jax
import jax.numpy as jnp
from jax import lax
from jax.sharding import PartitionSpec as P

HEAD_DIM = 128
KV_HEADS = 4
PASSAGE = 56
PASSAGES_DEV = 16
TOK_DEV = 896
SEL_DEV = 112
Q_WIDTH = 2048
KV_WIDTH = 1024
GROUP = 4


def update(carry_state, query_rows, query_pos, key_rows, value_rows, key_pos):
    running_max, weight_sum, summed = carry_state
    row_count = query_rows.shape[0]
    score_scale = HEAD_DIM ** (-0.5)
    query_split = query_rows.reshape(row_count, KV_HEADS, GROUP, HEAD_DIM)
    scores = (
        jnp.einsum("qkgd,pkd->qkgp", query_split, key_rows, preferred_element_type=jnp.float32)
        * score_scale
    )
    visible = key_pos[None, None, None, :] <= query_pos[:, None, None, None]
    scores = jnp.where(visible, scores, -1e30)
    new_max = jnp.maximum(running_max, jnp.max(scores, axis=-1))
    weights = jnp.where(visible, jnp.exp(scores - new_max[..., None]), 0.0)
    rescale = jnp.exp(running_max - new_max)
    weight_sum = weight_sum * rescale + jnp.sum(weights, axis=-1)
    product = jnp.einsum(
        "qkgp,pkd->qkgd",
        weights.astype(jnp.bfloat16),
        value_rows,
        preferred_element_type=jnp.float32,
    )
    summed = summed * rescale[..., None] + product
    return (new_max, weight_sum, summed)


def fold_attention(groups, blended):
    initial = []
    for query_rows, query_pos in groups:
        row_count = query_rows.shape[0]
        initial.append(
            (
                jnp.full((row_count, KV_HEADS, GROUP), -1e30, jnp.float32),
                jnp.zeros((row_count, KV_HEADS, GROUP), jnp.float32),
                jnp.zeros((row_count, KV_HEADS, GROUP, HEAD_DIM), jnp.float32),
            )
        )
    carry_all = tuple(initial)
    piece = lax.all_gather(blended, "seq", axis=0, tiled=True)
    absorb_row_count = piece.shape[0]
    block_rows = 512

    def take_block(state_all, step_index):
        key_part = lax.dynamic_slice_in_dim(piece, step_index * block_rows, block_rows, 0)
        first_pos = step_index * block_rows
        key_rows = key_part[:, : KV_HEADS * HEAD_DIM].reshape(block_rows, KV_HEADS, HEAD_DIM)
        value_rows = key_part[:, KV_HEADS * HEAD_DIM :].reshape(block_rows, KV_HEADS, HEAD_DIM)
        key_pos = first_pos + jnp.arange(block_rows, dtype=jnp.int32)
        updated = []
        for (query_rows, query_pos), carry_state in zip(groups, state_all):
            updated.append(
                lax.cond(
                    first_pos <= jnp.max(query_pos),
                    lambda state_in: update(
                        state_in, query_rows, query_pos, key_rows, value_rows, key_pos
                    ),
                    lambda state_in: state_in,
                    carry_state,
                )
            )
        return (tuple(updated), None)

    carry_all, _ = lax.scan(take_block, carry_all, jnp.arange(absorb_row_count // block_rows))
    finished = []
    for (query_rows, query_pos), carry_state in zip(groups, carry_all):
        row_count = query_rows.shape[0]
        output_rows = carry_state[2] / carry_state[1][..., None]
        finished.append(output_rows.reshape(row_count, Q_WIDTH).astype(jnp.bfloat16))
    return finished


def body(store, passage_owner, passage_slot, sel_pos, queries, new_kv):
    req_index = lax.axis_index("req")
    seq_index = lax.axis_index("seq")
    owner_table = passage_owner[:, :, 0]
    my_owner = lax.dynamic_index_in_dim(owner_table, req_index, 0, keepdims=False)
    store_shard = store[:, 0]
    req_count = owner_table.shape[0]
    owner_cap = max(2, (2 * PASSAGES_DEV + req_count - 1) // req_count)
    earlier = jnp.arange(PASSAGES_DEV)[:, None] > jnp.arange(PASSAGES_DEV)[None, :]
    same_owner = owner_table[:, :, None] == owner_table[:, None, :]
    rank_table = jnp.sum(same_owner & earlier[None], axis=2)
    slot_hit = (owner_table == req_index)[:, :, None] & (
        rank_table[:, :, None] == jnp.arange(owner_cap)[None, None, :]
    )
    send_slot = jnp.sum(jnp.where(slot_hit, passage_slot[:, :, None], 0), axis=1)
    outgoing = jnp.take(store_shard, send_slot.reshape(-1), axis=0)
    outgoing = outgoing.reshape(req_count, owner_cap, PASSAGE, KV_WIDTH)
    incoming = lax.all_to_all(outgoing, "req", split_axis=0, concat_axis=0, tiled=True)
    my_rank = lax.dynamic_index_in_dim(rank_table, req_index, 0, keepdims=False)
    flat_slot = my_owner * owner_cap + my_rank
    cached = jnp.take(incoming.reshape(req_count * owner_cap, PASSAGE, KV_WIDTH), flat_slot, axis=0)
    cached = cached.reshape(TOK_DEV, KV_WIDTH)
    all_pos = sel_pos[0]
    own_pos = lax.dynamic_slice_in_dim(all_pos, seq_index * SEL_DEV, SEL_DEV)
    offset = own_pos - seq_index * TOK_DEV
    fresh_rows = new_kv[0]
    picked = jnp.take(cached, offset, axis=0)
    blended = cached.at[offset].set(fresh_rows)
    difference = fresh_rows.astype(jnp.float32) - picked.astype(jnp.float32)
    squared = (difference * difference).reshape(SEL_DEV, 2, KV_HEADS, HEAD_DIM)
    deviation = jnp.sum(squared, axis=(1, 3))
    query_local = queries[0]
    attended = fold_attention([(query_local, own_pos)], blended)[0]
    return (blended[None], deviation[None], attended[None])


def solution(mesh):
    placed = (
        P("req", "seq", None, None),
        P(None, "seq", None),
        P(None, "seq"),
        P("req", None),
        P("req", "seq", None),
        P("req", "seq", None),
    )
    return jax.shard_map(
        body,
        mesh=mesh,
        in_specs=placed,
        out_specs=(P("req", "seq", None), P("req", "seq", None), P("req", "seq", None)),
        check_vma=False,
    )
```

profile of v0, /device:TPU:225, one launch (start us, length us, event | category | flops | bytes accessed | tf_op | source)
XLA Modules:
  0.0 505.5 jit_solution(7057776193855823319)
XLA Ops:
  17.2 6.8 %all-to-all-start = ((bf16[16,2,56,1024]{3,2,1,0:T(8,128)(2,1)}), bf16[16,2,56,1024]{3,2,1,0:T(8,128)(2,1)}, u32[]{:S(2)}, u32[]{:S(2)}) async-start(bf16[16,2,56,1024]{3,2,1,0:T(8,128)(2,1)} %broadcast_select_fusion), calls=%async_computation | async-start | bytes 7340032 | tf_op jit(solution)/shard_map/all_to_all | solution.py:104
  27.0 45.7 %all-to-all-done = bf16[16,2,56,1024]{3,2,1,0:T(8,128)(2,1)} async-done(((bf16[16,2,56,1024]{3,2,1,0:T(8,128)(2,1)}), bf16[16,2,56,1024]{3,2,1,0:T(8,128)(2,1)}, u32[]{:S(2)}, u32[]{:S(2)}) %all-to-all-start) | async-done | bytes 3670048 | tf_op jit(solution)/shard_map/all_to_all | solution.py:104
  84.1 158.5 %all-gather.2.cloned.1.call-done = bf16[14336,1024]{1,0:T(8,128)(2,1)} async-done(((bf16[896,1024]{1,0:T(8,128)(2,1)}), bf16[14336,1024]{1,0:T(8,128)(2,1)}) %all-gather.2.cloned.1.call-update) | async-done | bytes 29360144 | tf_op jit(solution)/shard_map/all_gather | solution.py:54
  242.6 35.1 %copy.27 = bf16[14336,1024]{0,1:T(8,128)(2,1)} copy(bf16[14336,1024]{1,0:T(8,128)(2,1)} %all-gather.2.cloned.1.call-done) | data formatting | bytes 58720256 | tf_op jit(solution)/shard_map/while | solution.py:78
  277.8 219.3 %while.15 = (s32[]{:T(128)}, f32[112,4,4]{0,2,1:T(4,128)S(1)}, f32[112,4,4]{0,2,1:T(4,128)S(1)}, f32[112,4,4,128]{3,0,2,1:T(8,128)S(1)}, s32[28]{0:T(128)S(1)}, ...) while((s32[]{:T(128)}, f32[112,4,4]{0,2,1:T(4,128)S(1)}, ...), condition=%wide.region_10.11_spmd, body=%wide.region_5.10_spmd.sunk | while | flops 482209792 | bytes 17720068 | solution.py:78
  279.7 5.9 %conditional.2 = ((f32[112,4,4]{0,2,1:T(4,128)S(1)}, f32[112,4,4]{0,2,1:T(4,128)S(1)}, f32[112,4,4,128]{3,0,2,1:T(8,128)S(1)})) conditional(s32[]{:T(128)} %convert_element_type.61, (f32[112,4,4]{0,2,1:T(4,128)S(1)}, f32[112,4,4]{0,2,1:T(4,128)S(1)}, f32[112,4,4,128]{3,0,2,1:T(8,128)S(1)}) %tuple.51, (s32[]{:T(128)}, s32[512]{0:T(512)S(1)}, ...), branch_computations={%region_6.6_spmd, %region_7.9_spmd} | conditional | flops 482209792 | bytes 17717786 | solution.py:67
  287.5 5.9 %conditional.2 = ((f32[112,4,4]{0,2,1:T(4,128)S(1)}, f32[112,4,4]{0,2,1:T(4,128)S(1)}, f32[112,4,4,128]{3,0,2,1:T(8,128)S(1)})) conditional(s32[]{:T(128)} %convert_element_type.61, (f32[112,4,4]{0,2,1:T(4,128)S(1)}, f32[112,4,4]{0,2,1:T(4,128)S(1)}, f32[112,4,4,128]{3,0,2,1:T(8,128)S(1)}) %tuple.51, (s32[]{:T(128)}, s32[512]{0:T(512)S(1)}, ...), branch_computations={%region_6.6_spmd, %region_7.9_spmd} | conditional | flops 482209792 | bytes 17717786 | solution.py:67
  295.4 5.9 %conditional.2 = ((f32[112,4,4]{0,2,1:T(4,128)S(1)}, f32[112,4,4]{0,2,1:T(4,128)S(1)}, f32[112,4,4,128]{3,0,2,1:T(8,128)S(1)})) conditional(s32[]{:T(128)} %convert_element_type.61, (f32[112,4,4]{0,2,1:T(4,128)S(1)}, f32[112,4,4]{0,2,1:T(4,128)S(1)}, f32[112,4,4,128]{3,0,2,1:T(8,128)S(1)}) %tuple.51, (s32[]{:T(128)}, s32[512]{0:T(512)S(1)}, ...), branch_computations={%region_6.6_spmd, %region_7.9_spmd} | conditional | flops 482209792 | bytes 17717786 | solution.py:67
  303.2 5.9 %conditional.2 = ((f32[112,4,4]{0,2,1:T(4,128)S(1)}, f32[112,4,4]{0,2,1:T(4,128)S(1)}, f32[112,4,4,128]{3,0,2,1:T(8,128)S(1)})) conditional(s32[]{:T(128)} %convert_element_type.61, (f32[112,4,4]{0,2,1:T(4,128)S(1)}, f32[112,4,4]{0,2,1:T(4,128)S(1)}, f32[112,4,4,128]{3,0,2,1:T(8,128)S(1)}) %tuple.51, (s32[]{:T(128)}, s32[512]{0:T(512)S(1)}, ...), branch_computations={%region_6.6_spmd, %region_7.9_spmd} | conditional | flops 482209792 | bytes 17717786 | solution.py:67
  311.0 5.9 %conditional.2 = ((f32[112,4,4]{0,2,1:T(4,128)S(1)}, f32[112,4,4]{0,2,1:T(4,128)S(1)}, f32[112,4,4,128]{3,0,2,1:T(8,128)S(1)})) conditional(s32[]{:T(128)} %convert_element_type.61, (f32[112,4,4]{0,2,1:T(4,128)S(1)}, f32[112,4,4]{0,2,1:T(4,128)S(1)}, f32[112,4,4,128]{3,0,2,1:T(8,128)S(1)}) %tuple.51, (s32[]{:T(128)}, s32[512]{0:T(512)S(1)}, ...), branch_computations={%region_6.6_spmd, %region_7.9_spmd} | conditional | flops 482209792 | bytes 17717786 | solution.py:67
  318.9 5.9 %conditional.2 = ((f32[112,4,4]{0,2,1:T(4,128)S(1)}, f32[112,4,4]{0,2,1:T(4,128)S(1)}, f32[112,4,4,128]{3,0,2,1:T(8,128)S(1)})) conditional(s32[]{:T(128)} %convert_element_type.61, (f32[112,4,4]{0,2,1:T(4,128)S(1)}, f32[112,4,4]{0,2,1:T(4,128)S(1)}, f32[112,4,4,128]{3,0,2,1:T(8,128)S(1)}) %tuple.51, (s32[]{:T(128)}, s32[512]{0:T(512)S(1)}, ...), branch_computations={%region_6.6_spmd, %region_7.9_spmd} | conditional | flops 482209792 | bytes 17717786 | solution.py:67
  326.7 5.9 %conditional.2 = ((f32[112,4,4]{0,2,1:T(4,128)S(1)}, f32[112,4,4]{0,2,1:T(4,128)S(1)}, f32[112,4,4,128]{3,0,2,1:T(8,128)S(1)})) conditional(s32[]{:T(128)} %convert_element_type.61, (f32[112,4,4]{0,2,1:T(4,128)S(1)}, f32[112,4,4]{0,2,1:T(4,128)S(1)}, f32[112,4,4,128]{3,0,2,1:T(8,128)S(1)}) %tuple.51, (s32[]{:T(128)}, s32[512]{0:T(512)S(1)}, ...), branch_computations={%region_6.6_spmd, %region_7.9_spmd} | conditional | flops 482209792 | bytes 17717786 | solution.py:67
  334.5 5.9 %conditional.2 = ((f32[112,4,4]{0,2,1:T(4,128)S(1)}, f32[112,4,4]{0,2,1:T(4,128)S(1)}, f32[112,4,4,128]{3,0,2,1:T(8,128)S(1)})) conditional(s32[]{:T(128)} %convert_element_type.61, (f32[112,4,4]{0,2,1:T(4,128)S(1)}, f32[112,4,4]{0,2,1:T(4,128)S(1)}, f32[112,4,4,128]{3,0,2,1:T(8,128)S(1)}) %tuple.51, (s32[]{:T(128)}, s32[512]{0:T(512)S(1)}, ...), branch_computations={%region_6.6_spmd, %region_7.9_spmd} | conditional | flops 482209792 | bytes 17717786 | solution.py:67
  342.4 5.9 %conditional.2 = ((f32[112,4,4]{0,2,1:T(4,128)S(1)}, f32[112,4,4]{0,2,1:T(4,128)S(1)}, f32[112,4,4,128]{3,0,2,1:T(8,128)S(1)})) conditional(s32[]{:T(128)} %convert_element_type.61, (f32[112,4,4]{0,2,1:T(4,128)S(1)}, f32[112,4,4]{0,2,1:T(4,128)S(1)}, f32[112,4,4,128]{3,0,2,1:T(8,128)S(1)}) %tuple.51, (s32[]{:T(128)}, s32[512]{0:T(512)S(1)}, ...), branch_computations={%region_6.6_spmd, %region_7.9_spmd} | conditional | flops 482209792 | bytes 17717786 | solution.py:67
  350.2 5.9 %conditional.2 = ((f32[112,4,4]{0,2,1:T(4,128)S(1)}, f32[112,4,4]{0,2,1:T(4,128)S(1)}, f32[112,4,4,128]{3,0,2,1:T(8,128)S(1)})) conditional(s32[]{:T(128)} %convert_element_type.61, (f32[112,4,4]{0,2,1:T(4,128)S(1)}, f32[112,4,4]{0,2,1:T(4,128)S(1)}, f32[112,4,4,128]{3,0,2,1:T(8,128)S(1)}) %tuple.51, (s32[]{:T(128)}, s32[512]{0:T(512)S(1)}, ...), branch_computations={%region_6.6_spmd, %region_7.9_spmd} | conditional | flops 482209792 | bytes 17717786 | solution.py:67
  358.0 5.9 %conditional.2 = ((f32[112,4,4]{0,2,1:T(4,128)S(1)}, f32[112,4,4]{0,2,1:T(4,128)S(1)}, f32[112,4,4,128]{3,0,2,1:T(8,128)S(1)})) conditional(s32[]{:T(128)} %convert_element_type.61, (f32[112,4,4]{0,2,1:T(4,128)S(1)}, f32[112,4,4]{0,2,1:T(4,128)S(1)}, f32[112,4,4,128]{3,0,2,1:T(8,128)S(1)}) %tuple.51, (s32[]{:T(128)}, s32[512]{0:T(512)S(1)}, ...), branch_computations={%region_6.6_spmd, %region_7.9_spmd} | conditional | flops 482209792 | bytes 17717786 | solution.py:67
  365.9 5.9 %conditional.2 = ((f32[112,4,4]{0,2,1:T(4,128)S(1)}, f32[112,4,4]{0,2,1:T(4,128)S(1)}, f32[112,4,4,128]{3,0,2,1:T(8,128)S(1)})) conditional(s32[]{:T(128)} %convert_element_type.61, (f32[112,4,4]{0,2,1:T(4,128)S(1)}, f32[112,4,4]{0,2,1:T(4,128)S(1)}, f32[112,4,4,128]{3,0,2,1:T(8,128)S(1)}) %tuple.51, (s32[]{:T(128)}, s32[512]{0:T(512)S(1)}, ...), branch_computations={%region_6.6_spmd, %region_7.9_spmd} | conditional | flops 482209792 | bytes 17717786 | solution.py:67
  373.7 5.9 %conditional.2 = ((f32[112,4,4]{0,2,1:T(4,128)S(1)}, f32[112,4,4]{0,2,1:T(4,128)S(1)}, f32[112,4,4,128]{3,0,2,1:T(8,128)S(1)})) conditional(s32[]{:T(128)} %convert_element_type.61, (f32[112,4,4]{0,2,1:T(4,128)S(1)}, f32[112,4,4]{0,2,1:T(4,128)S(1)}, f32[112,4,4,128]{3,0,2,1:T(8,128)S(1)}) %tuple.51, (s32[]{:T(128)}, s32[512]{0:T(512)S(1)}, ...), branch_computations={%region_6.6_spmd, %region_7.9_spmd} | conditional | flops 482209792 | bytes 17717786 | solution.py:67
  381.5 5.9 %conditional.2 = ((f32[112,4,4]{0,2,1:T(4,128)S(1)}, f32[112,4,4]{0,2,1:T(4,128)S(1)}, f32[112,4,4,128]{3,0,2,1:T(8,128)S(1)})) conditional(s32[]{:T(128)} %convert_element_type.61, (f32[112,4,4]{0,2,1:T(4,128)S(1)}, f32[112,4,4]{0,2,1:T(4,128)S(1)}, f32[112,4,4,128]{3,0,2,1:T(8,128)S(1)}) %tuple.51, (s32[]{:T(128)}, s32[512]{0:T(512)S(1)}, ...), branch_computations={%region_6.6_spmd, %region_7.9_spmd} | conditional | flops 482209792 | bytes 17717786 | solution.py:67
  389.4 5.9 %conditional.2 = ((f32[112,4,4]{0,2,1:T(4,128)S(1)}, f32[112,4,4]{0,2,1:T(4,128)S(1)}, f32[112,4,4,128]{3,0,2,1:T(8,128)S(1)})) conditional(s32[]{:T(128)} %convert_element_type.61, (f32[112,4,4]{0,2,1:T(4,128)S(1)}, f32[112,4,4]{0,2,1:T(4,128)S(1)}, f32[112,4,4,128]{3,0,2,1:T(8,128)S(1)}) %tuple.51, (s32[]{:T(128)}, s32[512]{0:T(512)S(1)}, ...), branch_computations={%region_6.6_spmd, %region_7.9_spmd} | conditional | flops 482209792 | bytes 17717786 | solution.py:67
  397.2 5.9 %conditional.2 = ((f32[112,4,4]{0,2,1:T(4,128)S(1)}, f32[112,4,4]{0,2,1:T(4,128)S(1)}, f32[112,4,4,128]{3,0,2,1:T(8,128)S(1)})) conditional(s32[]{:T(128)} %convert_element_type.61, (f32[112,4,4]{0,2,1:T(4,128)S(1)}, f32[112,4,4]{0,2,1:T(4,128)S(1)}, f32[112,4,4,128]{3,0,2,1:T(8,128)S(1)}) %tuple.51, (s32[]{:T(128)}, s32[512]{0:T(512)S(1)}, ...), branch_computations={%region_6.6_spmd, %region_7.9_spmd} | conditional | flops 482209792 | bytes 17717786 | solution.py:67
  405.0 5.9 %conditional.2 = ((f32[112,4,4]{0,2,1:T(4,128)S(1)}, f32[112,4,4]{0,2,1:T(4,128)S(1)}, f32[112,4,4,128]{3,0,2,1:T(8,128)S(1)})) conditional(s32[]{:T(128)} %convert_element_type.61, (f32[112,4,4]{0,2,1:T(4,128)S(1)}, f32[112,4,4]{0,2,1:T(4,128)S(1)}, f32[112,4,4,128]{3,0,2,1:T(8,128)S(1)}) %tuple.51, (s32[]{:T(128)}, s32[512]{0:T(512)S(1)}, ...), branch_computations={%region_6.6_spmd, %region_7.9_spmd} | conditional | flops 482209792 | bytes 17717786 | solution.py:67
  412.9 5.9 %conditional.2 = ((f32[112,4,4]{0,2,1:T(4,128)S(1)}, f32[112,4,4]{0,2,1:T(4,128)S(1)}, f32[112,4,4,128]{3,0,2,1:T(8,128)S(1)})) conditional(s32[]{:T(128)} %convert_element_type.61, (f32[112,4,4]{0,2,1:T(4,128)S(1)}, f32[112,4,4]{0,2,1:T(4,128)S(1)}, f32[112,4,4,128]{3,0,2,1:T(8,128)S(1)}) %tuple.51, (s32[]{:T(128)}, s32[512]{0:T(512)S(1)}, ...), branch_computations={%region_6.6_spmd, %region_7.9_spmd} | conditional | flops 482209792 | bytes 17717786 | solution.py:67
  420.7 5.9 %conditional.2 = ((f32[112,4,4]{0,2,1:T(4,128)S(1)}, f32[112,4,4]{0,2,1:T(4,128)S(1)}, f32[112,4,4,128]{3,0,2,1:T(8,128)S(1)})) conditional(s32[]{:T(128)} %convert_element_type.61, (f32[112,4,4]{0,2,1:T(4,128)S(1)}, f32[112,4,4]{0,2,1:T(4,128)S(1)}, f32[112,4,4,128]{3,0,2,1:T(8,128)S(1)}) %tuple.51, (s32[]{:T(128)}, s32[512]{0:T(512)S(1)}, ...), branch_computations={%region_6.6_spmd, %region_7.9_spmd} | conditional | flops 482209792 | bytes 17717786 | solution.py:67
  428.5 5.9 %conditional.2 = ((f32[112,4,4]{0,2,1:T(4,128)S(1)}, f32[112,4,4]{0,2,1:T(4,128)S(1)}, f32[112,4,4,128]{3,0,2,1:T(8,128)S(1)})) conditional(s32[]{:T(128)} %convert_element_type.61, (f32[112,4,4]{0,2,1:T(4,128)S(1)}, f32[112,4,4]{0,2,1:T(4,128)S(1)}, f32[112,4,4,128]{3,0,2,1:T(8,128)S(1)}) %tuple.51, (s32[]{:T(128)}, s32[512]{0:T(512)S(1)}, ...), branch_computations={%region_6.6_spmd, %region_7.9_spmd} | conditional | flops 482209792 | bytes 17717786 | solution.py:67
  436.4 5.9 %conditional.2 = ((f32[112,4,4]{0,2,1:T(4,128)S(1)}, f32[112,4,4]{0,2,1:T(4,128)S(1)}, f32[112,4,4,128]{3,0,2,1:T(8,128)S(1)})) conditional(s32[]{:T(128)} %convert_element_type.61, (f32[112,4,4]{0,2,1:T(4,128)S(1)}, f32[112,4,4]{0,2,1:T(4,128)S(1)}, f32[112,4,4,128]{3,0,2,1:T(8,128)S(1)}) %tuple.51, (s32[]{:T(128)}, s32[512]{0:T(512)S(1)}, ...), branch_computations={%region_6.6_spmd, %region_7.9_spmd} | conditional | flops 482209792 | bytes 17717786 | solution.py:67
  444.2 5.9 %conditional.2 = ((f32[112,4,4]{0,2,1:T(4,128)S(1)}, f32[112,4,4]{0,2,1:T(4,128)S(1)}, f32[112,4,4,128]{3,0,2,1:T(8,128)S(1)})) conditional(s32[]{:T(128)} %convert_element_type.61, (f32[112,4,4]{0,2,1:T(4,128)S(1)}, f32[112,4,4]{0,2,1:T(4,128)S(1)}, f32[112,4,4,128]{3,0,2,1:T(8,128)S(1)}) %tuple.51, (s32[]{:T(128)}, s32[512]{0:T(512)S(1)}, ...), branch_computations={%region_6.6_spmd, %region_7.9_spmd} | conditional | flops 482209792 | bytes 17717786 | solution.py:67
  452.0 5.9 %conditional.2 = ((f32[112,4,4]{0,2,1:T(4,128)S(1)}, f32[112,4,4]{0,2,1:T(4,128)S(1)}, f32[112,4,4,128]{3,0,2,1:T(8,128)S(1)})) conditional(s32[]{:T(128)} %convert_element_type.61, (f32[112,4,4]{0,2,1:T(4,128)S(1)}, f32[112,4,4]{0,2,1:T(4,128)S(1)}, f32[112,4,4,128]{3,0,2,1:T(8,128)S(1)}) %tuple.51, (s32[]{:T(128)}, s32[512]{0:T(512)S(1)}, ...), branch_computations={%region_6.6_spmd, %region_7.9_spmd} | conditional | flops 482209792 | bytes 17717786 | solution.py:67
  459.9 5.9 %conditional.2 = ((f32[112,4,4]{0,2,1:T(4,128)S(1)}, f32[112,4,4]{0,2,1:T(4,128)S(1)}, f32[112,4,4,128]{3,0,2,1:T(8,128)S(1)})) conditional(s32[]{:T(128)} %convert_element_type.61, (f32[112,4,4]{0,2,1:T(4,128)S(1)}, f32[112,4,4]{0,2,1:T(4,128)S(1)}, f32[112,4,4,128]{3,0,2,1:T(8,128)S(1)}) %tuple.51, (s32[]{:T(128)}, s32[512]{0:T(512)S(1)}, ...), branch_computations={%region_6.6_spmd, %region_7.9_spmd} | conditional | flops 482209792 | bytes 17717786 | solution.py:67
  467.7 5.9 %conditional.2 = ((f32[112,4,4]{0,2,1:T(4,128)S(1)}, f32[112,4,4]{0,2,1:T(4,128)S(1)}, f32[112,4,4,128]{3,0,2,1:T(8,128)S(1)})) conditional(s32[]{:T(128)} %convert_element_type.61, (f32[112,4,4]{0,2,1:T(4,128)S(1)}, f32[112,4,4]{0,2,1:T(4,128)S(1)}, f32[112,4,4,128]{3,0,2,1:T(8,128)S(1)}) %tuple.51, (s32[]{:T(128)}, s32[512]{0:T(512)S(1)}, ...), branch_computations={%region_6.6_spmd, %region_7.9_spmd} | conditional | flops 482209792 | bytes 17717786 | solution.py:67
  475.5 5.9 %conditional.2 = ((f32[112,4,4]{0,2,1:T(4,128)S(1)}, f32[112,4,4]{0,2,1:T(4,128)S(1)}, f32[112,4,4,128]{3,0,2,1:T(8,128)S(1)})) conditional(s32[]{:T(128)} %convert_element_type.61, (f32[112,4,4]{0,2,1:T(4,128)S(1)}, f32[112,4,4]{0,2,1:T(4,128)S(1)}, f32[112,4,4,128]{3,0,2,1:T(8,128)S(1)}) %tuple.51, (s32[]{:T(128)}, s32[512]{0:T(512)S(1)}, ...), branch_computations={%region_6.6_spmd, %region_7.9_spmd} | conditional | flops 482209792 | bytes 17717786 | solution.py:67
  483.4 5.9 %conditional.2 = ((f32[112,4,4]{0,2,1:T(4,128)S(1)}, f32[112,4,4]{0,2,1:T(4,128)S(1)}, f32[112,4,4,128]{3,0,2,1:T(8,128)S(1)})) conditional(s32[]{:T(128)} %convert_element_type.61, (f32[112,4,4]{0,2,1:T(4,128)S(1)}, f32[112,4,4]{0,2,1:T(4,128)S(1)}, f32[112,4,4,128]{3,0,2,1:T(8,128)S(1)}) %tuple.51, (s32[]{:T(128)}, s32[512]{0:T(512)S(1)}, ...), branch_computations={%region_6.6_spmd, %region_7.9_spmd} | conditional | flops 482209792 | bytes 17717786 | solution.py:67
  (386 shorter events, 212.5 us)
Async XLA Ops:
  7.2 3.2 copy-start
  17.2 55.5 %all-to-all-start = ((bf16[16,2,56,1024]{3,2,1,0:T(8,128)(2,1)}), bf16[16,2,56,1024]{3,2,1,0:T(8,128)(2,1)}, u32[]{:S(2)}, u32[]{:S(2)}) async-start(bf16[16,2,56,1024]{3,2,1,0:T(8,128)(2,1)} %broadcast_select_fusion), calls=%async_computation | async-start | bytes 7340032 | tf_op jit(solution)/shard_map/all_to_all | solution.py:104
  76.6 2.7 copy-start.4
  79.2 163.4 %all-gather.2.cloned.1.call-start = ((), (), s32[]{:S(2)}) async-start(), calls=%async_computation.1 | async-start | bytes 31195136 | tf_op jit(solution)/shard_map/all_gather | solution.py:54
  81.4 1.2 copy-start.2
  84.1 193.7 %copy-start.3 = (bf16[1,112,2048]{2,1,0:T(8,128)(2,1)S(1)}, bf16[1,112,2048]{2,1,0:T(8,128)(2,1)}, u32[]{:S(2)}) copy-start(bf16[1,112,2048]{2,1,0:T(8,128)(2,1)} %param.14) | copy-start | bytes 1376260
  497.0 1.6 copy-start.1
Sparse Core Ops, SparseCore 0:
  82.8 159.7 all-gather.1
where the time goes:
time: 508 us; the launch traced here: 506 us
  waiting for transfers between devices  204 us (40%)
  local copies, waits for them, and re-layouts  127 us (25%)
  matrix products  65.1 us (13%)
  other arithmetic  49.5 us (10%)
  loops' own time  38.6 us (8%)
  between operations  14.2 us (3%)
  starting transfers between devices  6.84 us (1%)
    all_gather x1, waiting for transfers between devices, fold_attention(): piece = lax.all_gather(blended, 'seq', axis=0, tiled=True)  159 us
    slice x28, local copies, waits for them, and re-layouts, take_block(): key_part[:, KV_HEADS * HEAD_DIM:].reshape(block_rows, KV_HEADS, HEAD_DIM)  52.1 us
    all_to_all x1, waiting for transfers between devices, body(): lax.all_to_all(outgoing, 'req', split_axis=0, concat_axis=0, tiled=True)  45.7 us
    dot_general x28, matrix products, update(): jnp.einsum('qkgp,pkd->qkgd', weights.astype(jnp.bfloat16), value_rows, pr...  42.1 us
    another operation x1, loops' own time, fold_attention(): lax.scan(take_block, carry_all, jnp.arange(absorb_row_count // block_rows))  36.9 us
    while x1, local copies, waits for them, and re-layouts, fold_attention(): lax.scan(take_block, carry_all, jnp.arange(absorb_row_count // block_rows))  35.1 us
    reduce_sum x28, other arithmetic, update(): weight_sum = weight_sum * rescale + jnp.sum(weights, axis=-1)  33.8 us
    dot_general x28, matrix products, update(): jnp.einsum('qkgd,pkd->qkgp', query_split, key_rows, preferred_element_typ...  23.1 us
  transfers between devices with their start and end apart: 2, of which 2 were waited for; matrix products, arithmetic and copies ran while one was open for 1% of the time, Pallas kernels for 0%

commit v1 on v0

v1 whole, which is shorter than its diff:
```python
import math

import jax
import jax.numpy as jnp
from jax import lax
from jax.experimental import pallas as pl
from jax.experimental.pallas import tpu as pltpu
from jax.sharding import PartitionSpec as P

NREQ = 16
NZ = 8
PIECES = 16
PASSAGE = 56
TOK = 896
SEL = 112
KVW = 1024
QW = 2048
D = 128
CHIP_TOK = 2 * TOK
C2 = (D ** -0.5) * math.log2(math.e)
EMPTY = -1e30
F32 = jnp.float32
BF16 = jnp.bfloat16
MESH = pl.DeviceIdType.MESH


def remote(src, dst, ssem, rsem, req, seq):
    return pltpu.make_async_remote_copy(
        src_ref=src,
        dst_ref=dst,
        send_sem=ssem,
        recv_sem=rsem,
        device_id=(req, seq),
        device_id_type=MESH,
    )


def kernel(
    owner, slot, pos, store, q, fresh_kv,
    blended_out, dev, att,
    outgoing, incoming, qh, qg, cached, blend, bh, kv, part, lse,
    buf_o, buf_l, fin,
    a_send, a_recv, qx_sem, qs_sem, qr_sem, kx_sem, ps_sem, pr_sem, fx_sem, b_sem,
):
    me = lax.axis_index("req")
    seq = lax.axis_index("seq")
    s = seq // 2
    c = seq % 2
    mate = s * 2 + (1 - c)
    above = lax.rem(s + 1, NZ) * 2 + c
    below = lax.rem(s + NZ - 1, NZ) * 2 + c

    def partner(i):
        return lax.rem(me + i, NREQ)

    barrier = pltpu.get_barrier_semaphore()
    for i in range(1, NREQ):
        pl.semaphore_signal(barrier, inc=1, device_id=(partner(i), seq), device_id_type=MESH)
    for z in (mate, above, below):
        pl.semaphore_signal(barrier, inc=1, device_id=(me, z), device_id_type=MESH)

    def build(r, carry):
        count = jnp.int32(0)
        first = jnp.int32(0)
        second = jnp.int32(0)
        for j in range(PIECES):
            hit = owner[r, j] == me
            value = slot[r, j]
            first = jnp.where(hit & (count == 0), value, first)
            second = jnp.where(hit & (count == 1), value, second)
            count = count + hit.astype(jnp.int32)
        outgoing[r, 0] = store[first]
        outgoing[r, 1] = store[second]
        return carry

    lax.fori_loop(0, NREQ, build, 0)
    for h in range(16):
        qh[h] = q[:, h * D : (h + 1) * D]
    pl.semaphore_wait(barrier, NREQ - 1 + 3)

    def a2a(i):
        return remote(
            outgoing.at[partner(i)], incoming.at[me], a_send.at[i], a_recv.at[i], partner(i), seq
        )

    def a2a_wait(i):
        src = lax.rem(me - i + NREQ, NREQ)
        return remote(
            outgoing.at[src], incoming.at[src], a_send.at[i], a_recv.at[i], src, seq
        )

    qx = remote(qh.at[pl.ds((1 - c) * 8, 8)], qg.at[s, :, c], qx_sem.at[0], qx_sem.at[1], me, mate)
    qx.start()
    order = [4, 12, 1, 3, 5, 13, 7, 15, 8, 2, 9, 6, 11, 14, 10]
    for i in order:
        a2a(i).start()
    incoming[me] = outgoing[me]
    for h in range(8):
        qg[s, h, c] = qh[c * 8 + h]
    remote(qh.at[pl.ds(0, 8)], qg.at[s, :, 1 - c], qx_sem.at[0], qx_sem.at[1], me, mate).wait_recv()

    def q_msg(z, t, up):
        if t == 4:
            ref = qg.at[z, pl.ds(4 if up else 0, 4)]
        else:
            ref = qg.at[z]
        k = 1 if up else 0
        return remote(ref, ref, qs_sem.at[k, t], qr_sem.at[k, t], me, above if up else below)

    for t in range(1, 5):
        z_down = s + t - 1
        z_up = lax.rem(s - t + 1 + NZ, NZ)
        if t > 1:

            @pl.when(z_down <= NZ - 1)
            def _(z=z_down, t=t):
                q_msg(z, t - 1, False).wait_recv()

        @pl.when((z_down <= NZ - 1) & (s >= 1))
        def _(z=z_down, t=t):
            q_msg(z, t, False).start()

        if t > 1:

            @pl.when(z_up >= 4)
            def _(z=z_up, t=t):
                q_msg(z, t - 1, True).wait_recv()

        @pl.when(z_up >= 4)
        def _(z=z_up, t=t):
            q_msg(z, t, True).start()

    eye = lax.broadcasted_iota(jnp.int32, (SEL, D), 0) == lax.broadcasted_iota(jnp.int32, (SEL, D), 1)

    def to_col(row):
        return jnp.sum(jnp.where(eye, row, 0.0), axis=1, keepdims=True)

    def to_row(col):
        return jnp.sum(jnp.where(eye, col, 0.0), axis=0, keepdims=True)

    own_row = pos[0:1, :]
    pick = (lax.broadcasted_iota(jnp.int32, (SEL, TOK), 1).astype(F32) == to_col(own_row)).astype(BF16)
    put = lax.broadcasted_iota(jnp.int32, (TOK, D), 0).astype(F32) == own_row
    hit_col = jnp.sum(jnp.where(put, 1.0, 0.0), axis=1, keepdims=True) > 0.5
    put = jnp.where(put, 1.0, 0.0).astype(BF16)[:, :SEL]

    for i in range(1, NREQ):
        a2a_wait(i).wait_recv()
    mine = [owner[me, j] for j in range(PIECES)]
    for j in range(PIECES):
        rank = jnp.int32(0)
        for k in range(j):
            rank = rank + (mine[k] == mine[j]).astype(jnp.int32)
        cached[j * PASSAGE : (j + 1) * PASSAGE, :] = incoming[mine[j], jnp.minimum(rank, 1)]

    squares = []
    for g in range(8):
        cols = slice(g * D, (g + 1) * D)
        old = cached[:, cols]
        new = fresh_kv[:, cols]
        placed = jnp.dot(put, new, preferred_element_type=F32)
        both = jnp.where(hit_col, placed, old.astype(F32)).astype(BF16)
        blend[:, cols] = both
        bh[g // 4, (g % 4) // 2, g % 2] = both
        picked = jnp.dot(pick, old, preferred_element_type=F32)
        diff = new.astype(F32) - picked
        squares.append(jnp.sum(diff * diff, axis=1, keepdims=True))
    kx = remote(bh.at[:, 1 - c], kv.at[:, :, c], kx_sem.at[0], kx_sem.at[1], me, mate)
    kx.start()
    out_copy = pltpu.make_async_copy(blend, blended_out, b_sem)
    out_copy.start()
    for k in range(2):
        for h in range(2):
            kv[k, h, c] = bh[k, c, h]
    for h in range(4):
        dev[:, h : h + 1] = squares[h] + squares[4 + h]

    @pl.when(s + 4 <= NZ - 1)
    def _():
        q_msg(s + 4, 4, False).wait_recv()

    @pl.when(lax.rem(s + 4, NZ) >= 4)
    def _():
        q_msg(lax.rem(s + 4, NZ), 4, True).wait_recv()

    remote(bh.at[:, c], kv.at[:, :, 1 - c], kx_sem.at[0], kx_sem.at[1], me, mate).wait_recv()

    def attend(zd, masked):
        def half(step, carry):
            kvh = step // 2
            first = kvh * 4 + (step % 2) * 2
            rows = qg[zd, pl.ds(first, 2)].reshape(4 * SEL, D)
            keys = kv[0, kvh].reshape(CHIP_TOK, D)
            values = kv[1, kvh].reshape(CHIP_TOK, D)
            scores = lax.dot_general(
                rows, keys, (((1,), (1,)), ((), ())), preferred_element_type=F32
            )
            if masked:
                limit = [to_col(pos[1:2, :]), to_col(pos[2:3, :])]
                limit = jnp.concatenate(limit + limit, axis=0)
                index = lax.broadcasted_iota(jnp.int32, (4 * SEL, CHIP_TOK), 1).astype(F32)
                scores = jnp.where(index <= limit, scores, EMPTY)
            top = jnp.max(scores, axis=1, keepdims=True)
            weights = jnp.exp2((scores - top) * C2)
            total = jnp.sum(weights, axis=1, keepdims=True)
            product = jnp.dot(weights.astype(BF16), values, preferred_element_type=F32)
            result = (product / total).astype(BF16)
            part[zd, pl.ds(first, 2)] = result.reshape(2, 2, SEL, D)
            level = top * C2 + jnp.log2(total)
            for g in range(4):
                lse[zd, kvh, pl.ds((step % 2) * 4 + g, 1), :] = to_row(level[g * SEL : (g + 1) * SEL])
            return carry

        lax.fori_loop(0, 4, half, 0)

    def merge(zd, kvh, k, slot_at):
        have = lse[zd, kvh]
        came = buf_l[k, slot_at, kvh]
        high = jnp.maximum(have, came)
        e_have = jnp.exp2(have - high)
        e_came = jnp.exp2(came - high)
        total = e_have + e_came
        share = e_came / total
        for g in range(4):
            for b in range(2):
                w = to_col(share[g * 2 + b : g * 2 + b + 1, :])
                x = part[zd, kvh * 4 + g, b].astype(F32)
                y = buf_o[k, slot_at, kvh * 4 + g, b].astype(F32)
                part[zd, kvh * 4 + g, b] = (x + w * (y - x)).astype(BF16)
        lse[zd, kvh] = high + jnp.log2(total)

    def p_msgs(zd, d, k, peer, half):
        if half is None:
            o_src, o_dst = part.at[zd], buf_o.at[k, d - 1]
        else:
            o_src = part.at[zd, pl.ds(half * 4, 4)]
            o_dst = buf_o.at[k, d - 1, pl.ds(half * 4, 4)]
        return (
            remote(o_src, o_dst, ps_sem.at[k, d, 0], pr_sem.at[k, d - 1, 0], me, peer),
            remote(lse.at[zd], buf_l.at[k, d - 1], ps_sem.at[k, d, 1], pr_sem.at[k, d - 1, 1], me, peer),
        )

    far = lax.rem(s + 4, NZ)

    @pl.when(s <= 3)
    def _():
        attend(far, False)
        for k, peer in ((0, above), (1, below)):
            for m in p_msgs(far, 4, k, peer, k):
                m.start()

    def ring(i, carry):
        d = 3 - i // 2
        k = lax.rem(i, 2)
        up = k == 0
        zd = jnp.where(up, lax.rem(s + d, NZ), lax.rem(s - d + NZ, NZ))
        peer = jnp.where(up, above, below)
        active = jnp.where(up, s + d, jnp.where(zd >= 4, 0, NZ)) <= NZ - 1
        fresh = active & (zd > s)
        comes = active & ((k == 1) | (s >= 1))

        @pl.when(fresh)
        def _():
            attend(zd, False)

        @pl.when(active & (zd < s))
        def _():
            part[zd] = jnp.zeros((8, 2, SEL, D), BF16)
            lse[zd] = jnp.full((2, 8, D), EMPTY, F32)

        @pl.when(comes & (d == 3))
        def _():
            remote(
                part.at[zd, pl.ds(0, 4)], buf_o.at[k, 3, pl.ds(k * 4, 4)],
                ps_sem.at[k, d, 0], pr_sem.at[k, 3, 0], me, peer,
            ).wait_recv()
            remote(
                lse.at[zd], buf_l.at[k, 3], ps_sem.at[k, d, 1], pr_sem.at[k, 3, 1], me, peer
            ).wait_recv()
            merge(zd, k, k, 3)

        @pl.when(comes & (d < 3))
        def _():
            for m in p_msgs(zd, d + 1, k, peer, None):
                m.wait_recv()
            merge(zd, 0, k, d)
            merge(zd, 1, k, d)

        @pl.when(active)
        def _():
            for m in p_msgs(zd, d, k, peer, None):
                m.start()

        return carry

    lax.fori_loop(0, 6, ring, 0)
    attend(s, True)
    for k, cond in ((0, s >= 1), (1, s >= 4)):

        @pl.when(cond)
        def _(k=k):
            for m in p_msgs(s, 1, k, below, None):
                m.wait_recv()
            merge(s, 0, k, 0)
            merge(s, 1, k, 0)

    fx = remote(part.at[s, :, 1 - c], fin.at[pl.ds(c * 8, 8)], fx_sem.at[0], fx_sem.at[1], me, mate)
    fx.start()
    for h in range(8):
        fin[c * 8 + h] = part[s, h, c]
    remote(
        part.at[s, :, c], fin.at[pl.ds((1 - c) * 8, 8)], fx_sem.at[0], fx_sem.at[1], me, mate
    ).wait_recv()
    for h in range(16):
        att[:, h * D : (h + 1) * D] = fin[h]

    fx.wait_send()
    kx.wait_send()
    qx.wait_send()
    out_copy.wait()
    for i in range(1, NREQ):
        a2a(i).wait_send()
    for t in range(1, 5):
        z_down = s + t - 1
        z_up = lax.rem(s - t + 1 + NZ, NZ)

        @pl.when((z_down <= NZ - 1) & (s >= 1))
        def _(z=z_down, t=t):
            q_msg(z, t, False).wait_send()

        @pl.when(z_up >= 4)
        def _(z=z_up, t=t):
            q_msg(z, t, True).wait_send()

    @pl.when(s <= 3)
    def _():
        for k, peer in ((0, above), (1, below)):
            for m in p_msgs(far, 4, k, peer, k):
                m.wait_send()

    def drain(i, carry):
        d = 3 - i // 2
        k = lax.rem(i, 2)
        up = k == 0
        zd = jnp.where(up, lax.rem(s + d, NZ), lax.rem(s - d + NZ, NZ))
        active = jnp.where(up, s + d, jnp.where(zd >= 4, 0, NZ)) <= NZ - 1

        @pl.when(active)
        def _():
            for m in p_msgs(zd, d, k, above, None):
                m.wait_send()

        return carry

    lax.fori_loop(0, 6, drain, 0)


def body(store, passage_owner, passage_slot, sel_pos, queries, new_kv):
    seq = lax.axis_index("seq")
    chip = seq // 2
    core = seq % 2
    owner = passage_owner[:, :, 0]
    near = lax.dynamic_slice(sel_pos[0], (chip * 2 * SEL,), (2 * SEL,)).reshape(2, SEL) - chip * CHIP_TOK
    own = lax.dynamic_index_in_dim(near, core, 0, keepdims=True) - core * TOK
    pos = jnp.concatenate([own, near], axis=0)
    pos = jnp.pad(pos, ((0, 5), (0, D - SEL)), constant_values=-1).astype(F32)
    vmem = pl.BlockSpec(memory_space=pltpu.VMEM)
    smem = pl.BlockSpec(memory_space=pltpu.SMEM)
    dma = pltpu.SemaphoreType.DMA
    blended, deviation, attended = pl.pallas_call(
        kernel,
        out_shape=(
            jax.ShapeDtypeStruct((TOK, KVW), BF16),
            jax.ShapeDtypeStruct((SEL, 4), F32),
            jax.ShapeDtypeStruct((SEL, QW), BF16),
        ),
        in_specs=[smem, smem, vmem, vmem, vmem, vmem],
        out_specs=(pl.BlockSpec(memory_space=pl.ANY), vmem, vmem),
        scratch_shapes=[
            pltpu.VMEM((NREQ, 2, PASSAGE, KVW), BF16),
            pltpu.VMEM((NREQ, 2, PASSAGE, KVW), BF16),
            pltpu.VMEM((16, SEL, D), BF16),
            pltpu.VMEM((NZ, 8, 2, SEL, D), BF16),
            pltpu.VMEM((TOK, KVW), BF16),
            pltpu.VMEM((TOK, KVW), BF16),
            pltpu.VMEM((2, 2, 2, TOK, D), BF16),
            pltpu.VMEM((2, 2, 2, TOK, D), BF16),
            pltpu.VMEM((NZ, 8, 2, SEL, D), BF16),
            pltpu.VMEM((NZ, 2, 8, D), F32),
            pltpu.VMEM((2, 4, 8, 2, SEL, D), BF16),
            pltpu.VMEM((2, 4, 2, 8, D), F32),
            pltpu.VMEM((16, SEL, D), BF16),
            dma((NREQ,)),
            dma((NREQ,)),
            dma((2,)),
            dma((2, 5)),
            dma((2, 5)),
            dma((2,)),
            dma((2, 5, 2)),
            dma((2, 5, 2)),
            dma((2,)),
            dma,
        ],
        compiler_params=pltpu.CompilerParams(
            collective_id=0, has_side_effects=True, vmem_limit_bytes=60 * 1024 * 1024
        ),
    )(owner, passage_slot, pos, store[:, 0], queries[0], new_kv[0])
    return blended[None], deviation[None], attended[None]


def solution(mesh):
    placed = (
        P("req", "seq", None, None),
        P(None, "seq", None),
        P(None, "seq"),
        P("req", None),
        P("req", "seq", None),
        P("req", "seq", None),
    )
    return jax.shard_map(
        body,
        mesh=mesh,
        in_specs=placed,
        out_specs=(P("req", "seq", None), P("req", "seq", None), P("req", "seq", None)),
        check_vma=False,
    )
```

time: 508 us -> 153 us (0.30)
  the two profiles are of different devices: /device:TPU:225 before, /device:TPU:8 now
where the time goes in v1:
time: 153 us
  Pallas kernels  145 us (95%)
  local copies, waits for them, and re-layouts  5.25 us (3%)
    pallas_call x1, Pallas kernels, body(): pl.pallas_call(kernel, out_shape=(jax.ShapeDtypeStruct((TOK, KVW), BF16),...  145 us
    unnamed x5, local copies, waits for them, and re-layouts  5.17 us

profile of v1, /device:TPU:8, one launch (start us, length us, event | category | flops | bytes accessed | tf_op | source)
XLA Modules:
  0.0 152.7 jit_solution(16030010019617604031)
XLA Ops:
  0.7 0.8 subtract_reduce_fusion
  1.4 0.1 sub.22
  1.5 0.6 pad_convert_fusion.pos
  2.1 145.3 %shard_map.85 = (bf16[896,1024]{1,0:T(8,128)(2,1)}, f32[112,4]{1,0:T(8,128)}, bf16[112,2048]{1,0:T(8,128)(2,1)}) custom-call(s32[16,16]{1,0:T(8,128)} %bitcast.13, s32[16,16]{1,0:T(8,128)} %slot.1, f32[8,128]{1,0:T(8,128)} %pad_convert_fusion.pos, bf16[9,56,1024]{2,1,0:T(8,128)(2,1)} %bitcast.8, bf16[112,2048]{1,0:T(8,128)(2,1)} %bitcast.10, ...), custom_call_target="tpu_custom_call" | custom-call | tf_op jit(solution)/shard_map/pallas_call | solution.py:370
  147.5 1.5 copy.9
  149.0 0.0 copy-start
  149.0 2.9 %copy.12 = bf16[1,896,1024]{2,1,0:T(8,128)(2,1)} copy(bf16[1,896,1024]{2,1,0:T(8,128)(2,1)} %bitcast.7) | data formatting | bytes 3670016
  151.9 0.0 copy-done
  151.9 0.8 copy.13
  (2 shorter events, 0.0 us)
Async XLA Ops:
  149.0 2.9 %copy-start = (bf16[112,2048]{1,0:T(8,128)(2,1)S(1)}, bf16[112,2048]{1,0:T(8,128)(2,1)}, u32[]{:S(2)}) copy-start(bf16[112,2048]{1,0:T(8,128)(2,1)} %get-tuple-element.8) | copy-start | bytes 1376260

commit v2 on v1

v2 whole, which is shorter than its diff:
```python
import math

import jax
import jax.numpy as jnp
from jax import lax
from jax.experimental import pallas as pl
from jax.experimental.pallas import tpu as pltpu
from jax.sharding import PartitionSpec as P

NREQ = 16
NZ = 8
PIECES = 16
PASSAGE = 56
TOK = 896
SEL = 112
KVW = 1024
QW = 2048
D = 128
CHIP_TOK = 2 * TOK
C2 = (D ** -0.5) * math.log2(math.e)
EMPTY = -1e30
F32 = jnp.float32
BF16 = jnp.bfloat16
MESH = pl.DeviceIdType.MESH


def remote(src, dst, ssem, rsem, req, seq):
    return pltpu.make_async_remote_copy(
        src_ref=src,
        dst_ref=dst,
        send_sem=ssem,
        recv_sem=rsem,
        device_id=(req, seq),
        device_id_type=MESH,
    )


RELAYS = (
    ((2, 0), (3, 0), (3, 0)),
    ((0, 2), (0, 3), (0, 3)),
    ((2, 2), (3, 3), (3, 3)),
    ((2, 1), (3, 0), (3, 1)),
    ((1, 2), (1, 3), (0, 3)),
    ((2, 3), (3, 0), (3, 3)),
    ((3, 2), (3, 3), (0, 3)),
)
ROUTES = (
    (2, 2), (2, 0), (0, 2), (2, 1), (1, 2), (2, 3), (3, 2), (1, 1),
    (3, 3), (1, 3), (3, 1), (1, 0), (3, 0), (0, 1), (0, 3),
)
CHUNK = 256


def kernel(
    owner, slot, pos, store, q, fresh_kv,
    blended_out, dev, att,
    outgoing, incoming_0, incoming_1, relayed, qh, qg, cached, blend, bh, kv, part, lse, share,
    buf_o, buf_l, fin, squares,
    a_send, a_recv, l_send, l_recv, f_send, f_recv,
    qx_sem, qs_sem, qr_sem, kx_send, kx_recv, ps_sem, pr_sem, fx_sem, b_sem,
):
    incoming = (incoming_0, incoming_1)
    me = lax.axis_index("req")
    seq = lax.axis_index("seq")
    s = seq // 2
    c = seq % 2
    x = me // 4
    y = me % 4
    mate = s * 2 + (1 - c)
    above = lax.rem(s + 1, NZ) * 2 + c
    below = lax.rem(s + NZ - 1, NZ) * 2 + c

    def to(step):
        return lax.rem(x + step[0], 4) * 4 + lax.rem(y + step[1], 4)

    def back(step):
        return lax.rem(x + 4 - step[0], 4) * 4 + lax.rem(y + 4 - step[1], 4)

    barrier = pltpu.get_barrier_semaphore()
    for step in ROUTES:
        pl.semaphore_signal(barrier, inc=1, device_id=(to(step), seq), device_id_type=MESH)
    for z in (mate, above, below):
        pl.semaphore_signal(barrier, inc=1, device_id=(me, z), device_id_type=MESH)

    for h in range(16):
        qh[h] = q[:, h * D : (h + 1) * D]

    def build(r, carry):
        count = jnp.int32(0)
        first = jnp.int32(0)
        second = jnp.int32(0)
        for j in range(PIECES):
            hit = owner[r, j] == me
            value = slot[r, j]
            first = jnp.where(hit & (count == 0), value, first)
            second = jnp.where(hit & (count == 1), value, second)
            count = count + hit.astype(jnp.int32)
        for k, at in ((0, first), (1, second)):
            piece = store[at]
            for p in range(2):
                for i in range(4):
                    col = (i % 2) * 512 + ((i // 2) * 2 + p) * D
                    outgoing[p, r, k, :, i * D : (i + 1) * D] = piece[:, col : col + D]
        return carry

    lax.fori_loop(0, NREQ, build, 0)
    pl.semaphore_wait(barrier, NREQ - 1 + 3)

    def direct(p, i, arriving):
        step = ROUTES[i]
        other = back(step) if arriving else to(step)
        row = other if arriving else me
        if 2 in step:
            o, n = outgoing.at[p, other, 0], incoming[p].at[row, 0]
        else:
            o, n = outgoing.at[p, other], incoming[p].at[row]
        return remote(o, n, a_send.at[p, i], a_recv.at[p, i], other, seq)

    def leg_one(p, i, arriving):
        target, leg, _ = RELAYS[i]
        other = back(leg) if arriving else to(leg)
        return remote(
            outgoing.at[p, to(target), 1], relayed.at[p, i], l_send.at[p, i], l_recv.at[p, i], other, seq
        )

    def leg_two(p, i, arriving):
        target, leg, last = RELAYS[i]
        other = back(last) if arriving else to(last)
        row = back(target) if arriving else back(leg)
        return remote(
            relayed.at[p, i], incoming[p].at[row, 1], f_send.at[p, i], f_recv.at[p, i], other, seq
        )

    def exchange_start(p):
        for i in range(len(RELAYS)):
            leg_one(p, i, False).start()
        for i in range(len(ROUTES)):
            direct(p, i, False).start()

    def exchange_pass(p):
        for i in range(len(RELAYS)):
            leg_one(p, i, True).wait_recv()
            leg_two(p, i, False).start()

    def q_msg(p, z, t, up):
        k = 1 if up else 0
        if t == 4:
            ref = qg.at[z, pl.ds(p * 4 + 2 * k, 2)]
        else:
            ref = qg.at[z, pl.ds(p * 4, 4)]
        return remote(ref, ref, qs_sem.at[p, k, t], qr_sem.at[p, k, t], me, above if up else below)

    def q_arrive(p, t):
        z_down = s + t
        z_up = lax.rem(s - t + NZ, NZ)

        @pl.when(z_down <= NZ - 1)
        def _():
            q_msg(p, z_down, t, False).wait_recv()

        @pl.when(z_up >= 4)
        def _():
            q_msg(p, z_up, t, True).wait_recv()

    def q_leave(p, t, over):
        z_down = s + t - 1
        z_up = lax.rem(s - t + 1 + NZ, NZ)

        @pl.when((z_down <= NZ - 1) & (s >= 1))
        def _():
            m = q_msg(p, z_down, t, False)
            m.wait_send() if over else m.start()

        @pl.when(z_up >= 4)
        def _():
            m = q_msg(p, z_up, t, True)
            m.wait_send() if over else m.start()

    qx = remote(qh.at[pl.ds((1 - c) * 8, 8)], qg.at[s, :, c], qx_sem.at[0], qx_sem.at[1], me, mate)
    qx.start()
    exchange_start(0)
    for h in range(8):
        qg[s, h, c] = qh[c * 8 + h]
    remote(qh.at[pl.ds(0, 8)], qg.at[s, :, 1 - c], qx_sem.at[0], qx_sem.at[1], me, mate).wait_recv()
    q_leave(0, 1, False)
    for p in range(2):
        incoming[p][me] = outgoing[p, me]

    eye = lax.broadcasted_iota(jnp.int32, (SEL, D), 0) == lax.broadcasted_iota(jnp.int32, (SEL, D), 1)

    def to_col(row):
        return jnp.sum(jnp.where(eye, row, 0.0), axis=1, keepdims=True)

    def to_row(col):
        return jnp.sum(jnp.where(eye, col, 0.0), axis=0, keepdims=True)

    exchange_pass(0)
    exchange_start(1)
    for t in range(2, 5):
        q_arrive(0, t - 1)
        q_leave(0, t, False)
    q_leave(1, 1, False)
    q_arrive(0, 4)

    def gathered(p):
        for i in range(len(ROUTES)):
            direct(p, i, True).wait_recv()
        for i in range(len(RELAYS)):
            leg_two(p, i, True).wait_recv()
        mine = [owner[me, j] for j in range(PIECES)]
        for j in range(PIECES):
            rank = jnp.int32(0)
            for k in range(j):
                rank = rank + (mine[k] == mine[j]).astype(jnp.int32)
            cached[j * PASSAGE : (j + 1) * PASSAGE, :] = incoming[p][mine[j], jnp.minimum(rank, 1)]

    def blend_in(p):
        own_row = pos[0:1, :]
        index = lax.broadcasted_iota(jnp.int32, (SEL, TOK), 1).astype(F32)
        pick = jnp.where(index == to_col(own_row), 1.0, 0.0).astype(BF16)
        put = jnp.where(lax.broadcasted_iota(jnp.int32, (TOK, D), 0).astype(F32) == own_row, 1.0, 0.0)
        hit_col = jnp.sum(put, axis=1, keepdims=True) > 0.5
        put = put.astype(BF16)[:, :SEL]
        for core in range(2):
            total = None
            for k in range(2):
                cols = pl.ds(pl.multiple_of(k * 512 + (core * 2 + p) * D, D), D)
                old = cached[:, (core * 2 + k) * D : (core * 2 + k + 1) * D]
                new = fresh_kv[:, cols]
                placed = jnp.dot(put, new, preferred_element_type=F32)
                both = jnp.where(hit_col, placed, old.astype(F32)).astype(BF16)
                blend[:, cols] = both
                bh[p, core, k] = both
                diff = new.astype(F32) - jnp.dot(pick, old, preferred_element_type=F32)
                total = diff * diff if total is None else total + diff * diff
            squares[core * 2 + p] = total

    def keys_msg(p, arriving):
        if arriving:
            return remote(bh.at[p, c], kv.at[p, :, 1 - c], kx_send.at[p], kx_recv.at[p], me, mate)
        return remote(bh.at[p, 1 - c], kv.at[p, :, c], kx_send.at[p], kx_recv.at[p], me, mate)

    def attend(zd, p, masked):
        rows = qg[zd, pl.ds(p * 4, 4)].reshape(8 * SEL, D)
        if masked:
            limit = [to_col(pos[1:2, :]), to_col(pos[2:3, :])]
            limit = jnp.concatenate(limit * 4, axis=0)
        top = total = product = None
        for i in range(CHIP_TOK // CHUNK):
            at = i * CHUNK
            keys = [kv[p, 0].reshape(CHIP_TOK, D)[at : at + CHUNK], kv[p, 1].reshape(CHIP_TOK, D)[at : at + CHUNK]]
            scores = lax.dot_general(
                rows, keys[0], (((1,), (1,)), ((), ())), preferred_element_type=F32
            )
            if masked:
                index = lax.broadcasted_iota(jnp.int32, (8 * SEL, CHUNK), 1).astype(F32) + float(at)
                scores = jnp.where(index <= limit, scores, EMPTY)
            high = jnp.max(scores, axis=1, keepdims=True)
            if top is not None:
                high = jnp.maximum(top, high)
            weights = jnp.exp2((scores - high) * C2)
            sums = weights[:, :D] + weights[:, D:]
            now = jnp.dot(weights.astype(BF16), keys[1], preferred_element_type=F32)
            if top is None:
                total, product = sums, now
            else:
                shrink = jnp.exp2((top - high) * C2)
                total = total * shrink + sums
                product = product * shrink + now
            top = high
        total = jnp.sum(total, axis=1, keepdims=True)
        part[zd, pl.ds(p * 4, 4)] = (product / total).astype(BF16).reshape(4, 2, SEL, D)
        level = top * C2 + jnp.log2(total)
        for g in range(8):
            lse[zd, p, g : g + 1, :] = to_row(level[g * SEL : (g + 1) * SEL])

    def merge(zd, p, k, at, half):
        have = lse[zd, p]
        came = buf_l[k, at, p]
        if half:
            row = lax.broadcasted_iota(jnp.int32, (8, D), 0) // 4
            came = jnp.where(row == k, came, EMPTY)
        high = jnp.maximum(have, came)
        e_have = jnp.exp2(have - high)
        e_came = jnp.exp2(came - high)
        total = e_have + e_came
        share[...] = e_came / total
        lse[zd, p] = high + jnp.log2(total)

        def one(g, carry):
            for b in range(2):
                w = to_col(share[pl.ds(g * 2 + b, 1), :])
                a = part[zd, p * 4 + g, b].astype(F32)
                n = buf_o[k, at, p * 4 + g, b].astype(F32)
                part[zd, p * 4 + g, b] = (a + w * (n - a)).astype(BF16)
            return carry

        if half:
            for g in range(2):
                one(k * 2 + g, 0)
        else:
            for g in range(4):
                one(g, 0)

    def p_msgs(zd, p, d, k, peer, half):
        heads = pl.ds(p * 4 + k * 2, 2) if half else pl.ds(p * 4, 4)
        return (
            remote(
                part.at[zd, heads], buf_o.at[k, d - 1, heads],
                ps_sem.at[p, k, d, 0], pr_sem.at[p, k, d - 1, 0], me, peer,
            ),
            remote(
                lse.at[zd, p], buf_l.at[k, d - 1, p],
                ps_sem.at[p, k, d, 1], pr_sem.at[p, k, d - 1, 1], me, peer,
            ),
        )

    far = lax.rem(s + 4, NZ)

    def phase(p, whole):
        for n in range(2):

            @pl.when(p == n)
            def _(n=n):
                gathered(n)

        blend_in(p)
        keys_msg(p, False).start()
        for k in range(2):
            kv[p, k, c] = bh[p, c, k]

        @pl.when(p == 0)
        def _():
            exchange_pass(1)

        @pl.when(p == 1)
        def _():
            q_arrive(1, 4)

        keys_msg(p, True).wait_recv()

        @pl.when(s <= 3)
        def _():
            attend(far, p, False)
            for k, peer in ((0, above), (1, below)):
                for m in p_msgs(far, p, 4, k, peer, True):
                    m.start()

        def ring(i, carry):
            d = 3 - i // 2
            k = lax.rem(i, 2)
            up = k == 0
            zd = jnp.where(up, lax.rem(s + d, NZ), lax.rem(s - d + NZ, NZ))
            peer = jnp.where(up, above, below)
            active = jnp.where(up, s + d, jnp.where(zd >= 4, 0, NZ)) <= NZ - 1
            comes = active & ((k == 1) | (s >= 1))

            for n in range(3):

                @pl.when((p == 0) & (i == 2 * n))
                def _(n=n):
                    q_arrive(1, n + 1)
                    q_leave(1, n + 2, False)

            @pl.when(active & (zd > s))
            def _():
                attend(zd, p, False)

            @pl.when(active & (zd < s))
            def _():
                part[zd, pl.ds(p * 4, 4)] = jnp.zeros((4, 2, SEL, D), BF16)
                lse[zd, p] = jnp.full((8, D), EMPTY, F32)

            @pl.when(comes & (d == 3))
            def _():
                for m in p_msgs(zd, p, 4, k, peer, True):
                    m.wait_recv()
                merge(zd, p, k, 3, True)

            @pl.when(comes & (d < 3))
            def _():
                for m in p_msgs(zd, p, d + 1, k, peer, False):
                    m.wait_recv()
                merge(zd, p, k, d, False)

            @pl.when(active)
            def _():
                for m in p_msgs(zd, p, d, k, peer, False):
                    m.start()

            return carry

        lax.fori_loop(0, 6, ring, 0)
        attend(s, p, True)
        return whole

    lax.fori_loop(0, 2, phase, 0)
    out_copy = pltpu.make_async_copy(blend, blended_out, b_sem)
    out_copy.start()
    for h in range(4):
        dev[:, h : h + 1] = jnp.sum(squares[h], axis=1, keepdims=True)

    def finish(p, carry):
        for k, cond in ((0, s >= 1), (1, s >= 4)):

            @pl.when(cond)
            def _(k=k):
                for m in p_msgs(s, p, 1, k, below, False):
                    m.wait_recv()
                merge(s, p, k, 0, False)

        return carry

    lax.fori_loop(0, 2, finish, 0)
    fx = remote(part.at[s, :, 1 - c], fin.at[pl.ds(c * 8, 8)], fx_sem.at[0], fx_sem.at[1], me, mate)
    fx.start()
    for h in range(8):
        fin[c * 8 + h] = part[s, h, c]

    def drain(p, carry):
        keys_msg(p, False).wait_send()
        for t in range(1, 5):
            q_leave(p, t, True)

        @pl.when(s <= 3)
        def _():
            for k, peer in ((0, above), (1, below)):
                for m in p_msgs(far, p, 4, k, peer, True):
                    m.wait_send()

        def sent(i, inner):
            d = 3 - i // 2
            k = lax.rem(i, 2)
            up = k == 0
            zd = jnp.where(up, lax.rem(s + d, NZ), lax.rem(s - d + NZ, NZ))
            active = jnp.where(up, s + d, jnp.where(zd >= 4, 0, NZ)) <= NZ - 1

            @pl.when(active)
            def _():
                for m in p_msgs(zd, p, d, k, above, False):
                    m.wait_send()

            return inner

        lax.fori_loop(0, 6, sent, 0)
        return carry

    lax.fori_loop(0, 2, drain, 0)
    for p in range(2):
        for i in range(len(ROUTES)):
            direct(p, i, False).wait_send()
        for i in range(len(RELAYS)):
            leg_one(p, i, False).wait_send()
            leg_two(p, i, False).wait_send()
    qx.wait_send()
    remote(
        part.at[s, :, c], fin.at[pl.ds((1 - c) * 8, 8)], fx_sem.at[0], fx_sem.at[1], me, mate
    ).wait_recv()
    for h in range(16):
        att[:, h * D : (h + 1) * D] = fin[h]
    fx.wait_send()
    out_copy.wait()


def body(store, passage_owner, passage_slot, sel_pos, queries, new_kv):
    seq = lax.axis_index("seq")
    chip = seq // 2
    core = seq % 2
    owner = passage_owner[:, :, 0]
    near = lax.dynamic_slice(sel_pos[0], (chip * 2 * SEL,), (2 * SEL,)).reshape(2, SEL) - chip * CHIP_TOK
    own = lax.dynamic_index_in_dim(near, core, 0, keepdims=True) - core * TOK
    pos = jnp.concatenate([own, near], axis=0)
    pos = jnp.pad(pos, ((0, 5), (0, D - SEL)), constant_values=-1).astype(F32)
    vmem = pl.BlockSpec(memory_space=pltpu.VMEM)
    smem = pl.BlockSpec(memory_space=pltpu.SMEM)
    dma = pltpu.SemaphoreType.DMA
    blended, deviation, attended = pl.pallas_call(
        kernel,
        out_shape=(
            jax.ShapeDtypeStruct((TOK, KVW), BF16),
            jax.ShapeDtypeStruct((SEL, 4), F32),
            jax.ShapeDtypeStruct((SEL, QW), BF16),
        ),
        in_specs=[smem, smem, vmem, vmem, vmem, vmem],
        out_specs=(pl.BlockSpec(memory_space=pl.ANY), vmem, vmem),
        scratch_shapes=[
            pltpu.VMEM((2, NREQ, 2, PASSAGE, KVW // 2), BF16),
            pltpu.VMEM((NREQ, 2, PASSAGE, KVW // 2), BF16),
            pltpu.VMEM((NREQ, 2, PASSAGE, KVW // 2), BF16),
            pltpu.VMEM((2, len(RELAYS), PASSAGE, KVW // 2), BF16),
            pltpu.VMEM((16, SEL, D), BF16),
            pltpu.VMEM((NZ, 8, 2, SEL, D), BF16),
            pltpu.VMEM((TOK, KVW // 2), BF16),
            pltpu.VMEM((TOK, KVW), BF16),
            pltpu.VMEM((2, 2, 2, TOK, D), BF16),
            pltpu.VMEM((2, 2, 2, TOK, D), BF16),
            pltpu.VMEM((NZ, 8, 2, SEL, D), BF16),
            pltpu.VMEM((NZ, 2, 8, D), F32),
            pltpu.VMEM((8, D), F32),
            pltpu.VMEM((2, 4, 8, 2, SEL, D), BF16),
            pltpu.VMEM((2, 4, 2, 8, D), F32),
            pltpu.VMEM((16, SEL, D), BF16),
            pltpu.VMEM((4, SEL, D), F32),
            dma((2, len(ROUTES))),
            dma((2, len(ROUTES))),
            dma((2, len(RELAYS))),
            dma((2, len(RELAYS))),
            dma((2, len(RELAYS))),
            dma((2, len(RELAYS))),
            dma((2,)),
            dma((2, 2, 5)),
            dma((2, 2, 5)),
            dma((2,)),
            dma((2,)),
            dma((2, 2, 5, 2)),
            dma((2, 2, 5, 2)),
            dma((2,)),
            dma,
        ],
        compiler_params=pltpu.CompilerParams(
            collective_id=0, has_side_effects=True, vmem_limit_bytes=60 * 1024 * 1024
        ),
    )(owner, passage_slot, pos, store[:, 0], queries[0], new_kv[0])
    return blended[None], deviation[None], attended[None]


def solution(mesh):
    placed = (
        P("req", "seq", None, None),
        P(None, "seq", None),
        P(None, "seq"),
        P("req", None),
        P("req", "seq", None),
        P("req", "seq", None),
    )
    return jax.shard_map(
        body,
        mesh=mesh,
        in_specs=placed,
        out_specs=(P("req", "seq", None), P("req", "seq", None), P("req", "seq", None)),
        check_vma=False,
    )
```

time: 153 us -> 122 us (0.80)
  Pallas kernels: 145 us -> 115 us
    pallas_call x1, Pallas kernels: 145 us -> 115 us  [body(): pl.pallas_call(kernel, out_shape=(jax.ShapeDtypeStruct((TOK, KVW), BF16),...]
where the time goes in v2:
time: 122 us
  Pallas kernels  115 us (94%)
  local copies, waits for them, and re-layouts  5.25 us (4%)
  other arithmetic  1.4 us (1%)
    pallas_call x1, Pallas kernels, body(): pl.pallas_call(kernel, out_shape=(jax.ShapeDtypeStruct((TOK, KVW), BF16),...  115 us
    unnamed x5, local copies, waits for them, and re-layouts  5.17 us

profile of v2, /device:TPU:8, one launch (start us, length us, event | category | flops | bytes accessed | tf_op | source)
XLA Modules:
  0.0 122.0 jit_solution(17398408238190531270)
XLA Ops:
  0.7 0.8 subtract_reduce_fusion
  1.4 0.1 sub.22
  1.5 0.6 pad_convert_fusion.pos
  2.1 114.7 %shard_map.85 = (bf16[896,1024]{1,0:T(8,128)(2,1)}, f32[112,4]{1,0:T(8,128)}, bf16[112,2048]{1,0:T(8,128)(2,1)}) custom-call(s32[16,16]{1,0:T(8,128)} %bitcast.13, s32[16,16]{1,0:T(8,128)} %slot.1, f32[8,128]{1,0:T(8,128)} %pad_convert_fusion.pos, bf16[9,56,1024]{2,1,0:T(8,128)(2,1)} %bitcast.8, bf16[112,2048]{1,0:T(8,128)(2,1)} %bitcast.10, ...), custom_call_target="tpu_custom_call" | custom-call | tf_op jit(solution)/shard_map/pallas_call | solution.py:477
  116.9 1.5 %copy.9 = f32[1,112,4]{1,2,0:T(4,128)} copy(f32[1,112,4]{2,1,0:T(8,128)} %bitcast.12) | data formatting | bytes 3584
  118.3 0.0 copy-start
  118.3 2.9 %copy.12 = bf16[1,896,1024]{2,1,0:T(8,128)(2,1)} copy(bf16[1,896,1024]{2,1,0:T(8,128)(2,1)} %bitcast.7) | data formatting | bytes 3670016
  121.3 0.0 copy-done
  121.3 0.8 copy.13
  (2 shorter events, 0.0 us)
Async XLA Ops:
  118.3 2.9 %copy-start = (bf16[112,2048]{1,0:T(8,128)(2,1)S(1)}, bf16[112,2048]{1,0:T(8,128)(2,1)}, u32[]{:S(2)}) copy-start(bf16[112,2048]{1,0:T(8,128)(2,1)} %get-tuple-element.8) | copy-start | bytes 1376260

commit v3 on v2

--- a/solution.py
+++ b/solution.py
@@ -35,18 +35,9 @@
     )
 
 
-RELAYS = (
-    ((2, 0), (3, 0), (3, 0)),
-    ((0, 2), (0, 3), (0, 3)),
-    ((2, 2), (3, 3), (3, 3)),
-    ((2, 1), (3, 0), (3, 1)),
-    ((1, 2), (1, 3), (0, 3)),
-    ((2, 3), (3, 0), (3, 3)),
-    ((3, 2), (3, 3), (0, 3)),
-)
 ROUTES = (
-    (2, 2), (2, 0), (0, 2), (2, 1), (1, 2), (2, 3), (3, 2), (1, 1),
-    (3, 3), (1, 3), (3, 1), (1, 0), (3, 0), (0, 1), (0, 3),
+    (1, 0), (3, 0), (0, 1), (0, 3), (2, 0), (0, 2), (1, 1), (3, 3),
+    (1, 3), (3, 1), (2, 1), (1, 2), (2, 3), (3, 2), (2, 2),
 )
 CHUNK = 256
 
@@ -54,9 +45,9 @@
 def kernel(
     owner, slot, pos, store, q, fresh_kv,
     blended_out, dev, att,
-    outgoing, incoming_0, incoming_1, relayed, qh, qg, cached, blend, bh, kv, part, lse, share,
+    outgoing, incoming_0, incoming_1, qh, qg, cached, blend, bh, kv, part, lse,
     buf_o, buf_l, fin, squares,
-    a_send, a_recv, l_send, l_recv, f_send, f_recv,
+    a_send, a_recv,
     qx_sem, qs_sem, qr_sem, kx_send, kx_recv, ps_sem, pr_sem, fx_sem, b_sem,
 ):
     incoming = (incoming_0, incoming_1)
@@ -71,10 +62,12 @@
     below = lax.rem(s + NZ - 1, NZ) * 2 + c
 
     def to(step):
-        return lax.rem(x + step[0], 4) * 4 + lax.rem(y + step[1], 4)
+        dx = jnp.where(c == 0, step[0], 4 - step[0])
+        dy = jnp.where(c == 0, step[1], 4 - step[1])
+        return lax.rem(x + dx, 4) * 4 + lax.rem(y + dy, 4)
 
     def back(step):
-        return lax.rem(x + 4 - step[0], 4) * 4 + lax.rem(y + 4 - step[1], 4)
+        return to((4 - step[0], 4 - step[1]))
 
     barrier = pltpu.get_barrier_semaphore()
     for step in ROUTES:
@@ -107,82 +100,64 @@
     pl.semaphore_wait(barrier, NREQ - 1 + 3)
 
     def direct(p, i, arriving):
-        step = ROUTES[i]
-        other = back(step) if arriving else to(step)
+        other = back(ROUTES[i]) if arriving else to(ROUTES[i])
         row = other if arriving else me
-        if 2 in step:
-            o, n = outgoing.at[p, other, 0], incoming[p].at[row, 0]
-        else:
-            o, n = outgoing.at[p, other], incoming[p].at[row]
-        return remote(o, n, a_send.at[p, i], a_recv.at[p, i], other, seq)
-
-    def leg_one(p, i, arriving):
-        target, leg, _ = RELAYS[i]
-        other = back(leg) if arriving else to(leg)
         return remote(
-            outgoing.at[p, to(target), 1], relayed.at[p, i], l_send.at[p, i], l_recv.at[p, i], other, seq
+            outgoing.at[p, other], incoming[p].at[row], a_send.at[p, i], a_recv.at[p, i], other, seq
         )
 
-    def leg_two(p, i, arriving):
-        target, leg, last = RELAYS[i]
-        other = back(last) if arriving else to(last)
-        row = back(target) if arriving else back(leg)
-        return remote(
-            relayed.at[p, i], incoming[p].at[row, 1], f_send.at[p, i], f_recv.at[p, i], other, seq
-        )
-
     def exchange_start(p):
-        for i in range(len(RELAYS)):
-            leg_one(p, i, False).start()
         for i in range(len(ROUTES)):
             direct(p, i, False).start()
 
-    def exchange_pass(p):
-        for i in range(len(RELAYS)):
-            leg_one(p, i, True).wait_recv()
-            leg_two(p, i, False).start()
-
-    def q_msg(p, z, t, up):
+    def q_msg(p, h, z, t, up):
         k = 1 if up else 0
-        if t == 4:
-            ref = qg.at[z, pl.ds(p * 4 + 2 * k, 2)]
-        else:
-            ref = qg.at[z, pl.ds(p * 4, 4)]
-        return remote(ref, ref, qs_sem.at[p, k, t], qr_sem.at[p, k, t], me, above if up else below)
-
-    def q_arrive(p, t):
+        ref = qg.at[z, pl.ds(p * 4 + 2 * h, 2)]
+        return remote(
+            ref, ref, qs_sem.at[p, h, k, t], qr_sem.at[p, h, k, t], me, above if up else below
+        )
+
+    def q_arrive(p, h, t):
         z_down = s + t
         z_up = lax.rem(s - t + NZ, NZ)
-
-        @pl.when(z_down <= NZ - 1)
-        def _():
-            q_msg(p, z_down, t, False).wait_recv()
-
-        @pl.when(z_up >= 4)
-        def _():
-            q_msg(p, z_up, t, True).wait_recv()
-
-    def q_leave(p, t, over):
+        if t < 4 or h == 0:
+
+            @pl.when(z_down <= NZ - 1)
+            def _():
+                q_msg(p, h, z_down, t, False).wait_recv()
+
+        if t < 4 or h == 1:
+
+            @pl.when(z_up >= 4)
+            def _():
+                q_msg(p, h, z_up, t, True).wait_recv()
+
+    def q_leave(p, h, t, over):
         z_down = s + t - 1
         z_up = lax.rem(s - t + 1 + NZ, NZ)
-
-        @pl.when((z_down <= NZ - 1) & (s >= 1))
-        def _():
-            m = q_msg(p, z_down, t, False)
-            m.wait_send() if over else m.start()
-
-        @pl.when(z_up >= 4)
-        def _():
-            m = q_msg(p, z_up, t, True)
-            m.wait_send() if over else m.start()
+        if t < 4 or h == 0:
+
+            @pl.when((z_down <= NZ - 1) & (s >= 1))
+            def _():
+                m = q_msg(p, h, z_down, t, False)
+                m.wait_send() if over else m.start()
+
+        if t < 4 or h == 1:
+
+            @pl.when(z_up >= 4)
+            def _():
+                m = q_msg(p, h, z_up, t, True)
+                m.wait_send() if over else m.start()
 
     qx = remote(qh.at[pl.ds((1 - c) * 8, 8)], qg.at[s, :, c], qx_sem.at[0], qx_sem.at[1], me, mate)
     qx.start()
     exchange_start(0)
+    exchange_start(1)
     for h in range(8):
         qg[s, h, c] = qh[c * 8 + h]
     remote(qh.at[pl.ds(0, 8)], qg.at[s, :, 1 - c], qx_sem.at[0], qx_sem.at[1], me, mate).wait_recv()
-    q_leave(0, 1, False)
+    for h in range(2):
+        q_leave(0, h, 1, False)
     for p in range(2):
         incoming[p][me] = outgoing[p, me]
 
@@ -194,19 +169,18 @@
     def to_row(col):
         return jnp.sum(jnp.where(eye, col, 0.0), axis=0, keepdims=True)
 
-    exchange_pass(0)
-    exchange_start(1)
     for t in range(2, 5):
-        q_arrive(0, t - 1)
-        q_leave(0, t, False)
-    q_leave(1, 1, False)
-    q_arrive(0, 4)
+        for h in range(2):
+            q_arrive(0, h, t - 1)
+            q_leave(0, h, t, False)
+    for h in range(2):
+        q_leave(1, h, 1, False)
+    for h in range(2):
+        q_arrive(0, h, 4)
 
     def gathered(p):
         for i in range(len(ROUTES)):
             direct(p, i, True).wait_recv()
-        for i in range(len(RELAYS)):
-            leg_two(p, i, True).wait_recv()
         mine = [owner[me, j] for j in range(PIECES)]
         for j in range(PIECES):
             rank = jnp.int32(0)
@@ -272,46 +246,34 @@
         part[zd, pl.ds(p * 4, 4)] = (product / total).astype(BF16).reshape(4, 2, SEL, D)
         level = top * C2 + jnp.log2(total)
         for g in range(8):
-            lse[zd, p, g : g + 1, :] = to_row(level[g * SEL : (g + 1) * SEL])
-
-    def merge(zd, p, k, at, half):
-        have = lse[zd, p]
-        came = buf_l[k, at, p]
-        if half:
-            row = lax.broadcasted_iota(jnp.int32, (8, D), 0) // 4
-            came = jnp.where(row == k, came, EMPTY)
+            lse[zd, p, g // 4, g % 4 : g % 4 + 1, :] = to_row(level[g * SEL : (g + 1) * SEL])
+
+    def merge(zd, p, k, at, h):
+        have = lse[zd, p, h]
+        came = buf_l[k, at, p, h]
         high = jnp.maximum(have, came)
         e_have = jnp.exp2(have - high)
         e_came = jnp.exp2(came - high)
         total = e_have + e_came
-        share[...] = e_came / total
-        lse[zd, p] = high + jnp.log2(total)
-
-        def one(g, carry):
+        part_of = e_came / total
+        lse[zd, p, h] = high + jnp.log2(total)
+        for g in range(2):
             for b in range(2):
-                w = to_col(share[pl.ds(g * 2 + b, 1), :])
-                a = part[zd, p * 4 + g, b].astype(F32)
-                n = buf_o[k, at, p * 4 + g, b].astype(F32)
-                part[zd, p * 4 + g, b] = (a + w * (n - a)).astype(BF16)
-            return carry
-
-        if half:
-            for g in range(2):
-                one(k * 2 + g, 0)
-        else:
-            for g in range(4):
-                one(g, 0)
-
-    def p_msgs(zd, p, d, k, peer, half):
-        heads = pl.ds(p * 4 + k * 2, 2) if half else pl.ds(p * 4, 4)
+                w = to_col(part_of[g * 2 + b : g * 2 + b + 1, :])
+                a = part[zd, p * 4 + h * 2 + g, b].astype(F32)
+                n = buf_o[k, at, p * 4 + h * 2 + g, b].astype(F32)
+                part[zd, p * 4 + h * 2 + g, b] = (a + w * (n - a)).astype(BF16)
+
+    def p_msgs(zd, p, d, k, h, peer):
+        heads = pl.ds(p * 4 + h * 2, 2)
         return (
             remote(
                 part.at[zd, heads], buf_o.at[k, d - 1, heads],
-                ps_sem.at[p, k, d, 0], pr_sem.at[p, k, d - 1, 0], me, peer,
+                ps_sem.at[p, k, d, h, 0], pr_sem.at[p, k, d - 1, h, 0], me, peer,
             ),
             remote(
-                lse.at[zd, p], buf_l.at[k, d - 1, p],
-                ps_sem.at[p, k, d, 1], pr_sem.at[p, k, d - 1, 1], me, peer,
+                lse.at[zd, p, h], buf_l.at[k, d - 1, p, h],
+                ps_sem.at[p, k, d, h, 1], pr_sem.at[p, k, d - 1, h, 1], me, peer,
             ),
         )
 
@@ -329,13 +291,10 @@
         for k in range(2):
             kv[p, k, c] = bh[p, c, k]
 
-        @pl.when(p == 0)
-        def _():
-            exchange_pass(1)
-
         @pl.when(p == 1)
         def _():
-            q_arrive(1, 4)
+            for h in range(2):
+                q_arrive(1, h, 4)
 
         keys_msg(p, True).wait_recv()
 
@@ -343,7 +302,7 @@
         def _():
             attend(far, p, False)
             for k, peer in ((0, above), (1, below)):
-                for m in p_msgs(far, p, 4, k, peer, True):
+                for m in p_msgs(far, p, 4, k, k, peer):
                     m.start()
 
         def ring(i, carry):
@@ -359,8 +318,9 @@
 
                 @pl.when((p == 0) & (i == 2 * n))
                 def _(n=n):
-                    q_arrive(1, n + 1)
-                    q_leave(1, n + 2, False)
+                    for h in range(2):
+                        q_arrive(1, h, n + 1)
+                        q_leave(1, h, n + 2, False)
 
             @pl.when(active & (zd > s))
             def _():
@@ -369,25 +329,23 @@
             @pl.when(active & (zd < s))
             def _():
                 part[zd, pl.ds(p * 4, 4)] = jnp.zeros((4, 2, SEL, D), BF16)
-                lse[zd, p] = jnp.full((8, D), EMPTY, F32)
-
-            @pl.when(comes & (d == 3))
-            def _():
-                for m in p_msgs(zd, p, 4, k, peer, True):
-                    m.wait_recv()
-                merge(zd, p, k, 3, True)
-
-            @pl.when(comes & (d < 3))
-            def _():
-                for m in p_msgs(zd, p, d + 1, k, peer, False):
-                    m.wait_recv()
-                merge(zd, p, k, d, False)
-
-            @pl.when(active)
-            def _():
-                for m in p_msgs(zd, p, d, k, peer, False):
-                    m.start()
-
+                lse[zd, p] = jnp.full((2, 4, D), EMPTY, F32)
+
+            def pass_on(h, inner):
+                @pl.when(comes & ((d < 3) | (h == k)))
+                def _():
+                    for m in p_msgs(zd, p, d + 1, k, h, peer):
+                        m.wait_recv()
+                    merge(zd, p, k, d, h)
+
+                @pl.when(active)
+                def _():
+                    for m in p_msgs(zd, p, d, k, h, peer):
+                        m.start()
+
+                return inner
+
+            lax.fori_loop(0, 2, pass_on, 0)
             return carry
 
         lax.fori_loop(0, 6, ring, 0)
@@ -398,16 +356,17 @@
     out_copy = pltpu.make_async_copy(blend, blended_out, b_sem)
     out_copy.start()
     for h in range(4):
-        dev[:, h : h + 1] = jnp.sum(squares[h], axis=1, keepdims=True)
+        dev[h : h + 1, :] = to_row(jnp.sum(squares[h], axis=1, keepdims=True))[:, :SEL]
 
     def finish(p, carry):
         for k, cond in ((0, s >= 1), (1, s >= 4)):
 
             @pl.when(cond)
             def _(k=k):
-                for m in p_msgs(s, p, 1, k, below, False):
-                    m.wait_recv()
-                merge(s, p, k, 0, False)
+                for h in range(2):
+                    for m in p_msgs(s, p, 1, k, h, below):
+                        m.wait_recv()
+                    merge(s, p, k, 0, h)
 
         return carry
 
@@ -420,12 +379,13 @@
     def drain(p, carry):
         keys_msg(p, False).wait_send()
         for t in range(1, 5):
-            q_leave(p, t, True)
+            for h in range(2):
+                q_leave(p, h, t, True)
 
         @pl.when(s <= 3)
         def _():
             for k, peer in ((0, above), (1, below)):
-                for m in p_msgs(far, p, 4, k, peer, True):
+                for m in p_msgs(far, p, 4, k, k, peer):
                     m.wait_send()
 
         def sent(i, inner):
@@ -437,8 +397,9 @@
 
             @pl.when(active)
             def _():
-                for m in p_msgs(zd, p, d, k, above, False):
-                    m.wait_send()
+                for h in range(2):
+                    for m in p_msgs(zd, p, d, k, h, above):
+                        m.wait_send()
 
             return inner
 
@@ -449,9 +410,6 @@
     for p in range(2):
         for i in range(len(ROUTES)):
             direct(p, i, False).wait_send()
-        for i in range(len(RELAYS)):
-            leg_one(p, i, False).wait_send()
-            leg_two(p, i, False).wait_send()
     qx.wait_send()
     remote(
         part.at[s, :, c], fin.at[pl.ds((1 - c) * 8, 8)], fx_sem.at[0], fx_sem.at[1], me, mate
@@ -460,6 +418,19 @@
         att[:, h * D : (h + 1) * D] = fin[h]
     fx.wait_send()
     out_copy.wait()
+
+
+def hand_on(a_in, b_in, c_in, a_out, b_out, c_out, a_mid, b_mid, c_mid, sem_in, sem_out):
+    ways = ((a_in, a_mid, a_out), (b_in, b_mid, b_out), (c_in, c_mid, c_out))
+    taken = [pltpu.make_async_copy(w[0], w[1], sem_in.at[i]) for i, w in enumerate(ways)]
+    given = [pltpu.make_async_copy(w[1], w[2], sem_out.at[i]) for i, w in enumerate(ways)]
+    for copy in taken:
+        copy.start()
+    for first, then in zip(taken, given):
+        first.wait()
+        then.start()
+    for copy in given:
+        copy.wait()
 
 
 def body(store, passage_owner, passage_slot, sel_pos, queries, new_kv):
@@ -478,7 +449,7 @@
         kernel,
         out_shape=(
             jax.ShapeDtypeStruct((TOK, KVW), BF16),
-            jax.ShapeDtypeStruct((SEL, 4), F32),
+            jax.ShapeDtypeStruct((4, SEL), F32),
             jax.ShapeDtypeStruct((SEL, QW), BF16),
         ),
         in_specs=[smem, smem, vmem, vmem, vmem, vmem],
@@ -487,7 +458,6 @@
             pltpu.VMEM((2, NREQ, 2, PASSAGE, KVW // 2), BF16),
             pltpu.VMEM((NREQ, 2, PASSAGE, KVW // 2), BF16),
             pltpu.VMEM((NREQ, 2, PASSAGE, KVW // 2), BF16),
-            pltpu.VMEM((2, len(RELAYS), PASSAGE, KVW // 2), BF16),
             pltpu.VMEM((16, SEL, D), BF16),
             pltpu.VMEM((NZ, 8, 2, SEL, D), BF16),
             pltpu.VMEM((TOK, KVW // 2), BF16),
@@ -495,25 +465,20 @@
             pltpu.VMEM((2, 2, 2, TOK, D), BF16),
             pltpu.VMEM((2, 2, 2, TOK, D), BF16),
             pltpu.VMEM((NZ, 8, 2, SEL, D), BF16),
-            pltpu.VMEM((NZ, 2, 8, D), F32),
-            pltpu.VMEM((8, D), F32),
+            pltpu.VMEM((NZ, 2, 2, 4, D), F32),
             pltpu.VMEM((2, 4, 8, 2, SEL, D), BF16),
-            pltpu.VMEM((2, 4, 2, 8, D), F32),
+            pltpu.VMEM((2, 4, 2, 2, 4, D), F32),
             pltpu.VMEM((16, SEL, D), BF16),
             pltpu.VMEM((4, SEL, D), F32),
             dma((2, len(ROUTES))),
             dma((2, len(ROUTES))),
-            dma((2, len(RELAYS))),
-            dma((2, len(RELAYS))),
-            dma((2, len(RELAYS))),
-            dma((2, len(RELAYS))),
             dma((2,)),
-            dma((2, 2, 5)),
-            dma((2, 2, 5)),
+            dma((2, 2, 2, 5)),
+            dma((2, 2, 2, 5)),
             dma((2,)),
             dma((2,)),
-            dma((2, 2, 5, 2)),
-            dma((2, 2, 5, 2)),
+            dma((2, 2, 5, 2, 2)),
+            dma((2, 2, 5, 2, 2)),
             dma((2,)),
             dma,
         ],
@@ -521,7 +486,24 @@
             collective_id=0, has_side_effects=True, vmem_limit_bytes=60 * 1024 * 1024
         ),
     )(owner, passage_slot, pos, store[:, 0], queries[0], new_kv[0])
-    return blended[None], deviation[None], attended[None]
+    blended, deviation, attended = pl.pallas_call(
+        hand_on,
+        out_shape=(
+            jax.ShapeDtypeStruct((TOK, KVW), BF16),
+            jax.ShapeDtypeStruct((4, SEL), F32),
+            jax.ShapeDtypeStruct((SEL, QW), BF16),
+        ),
+        in_specs=[pl.BlockSpec(memory_space=pl.ANY)] * 3,
+        out_specs=(pl.BlockSpec(memory_space=pl.ANY),) * 3,
+        scratch_shapes=[
+            pltpu.VMEM((TOK, KVW), BF16),
+            pltpu.VMEM((4, SEL), F32),
+            pltpu.VMEM((SEL, QW), BF16),
+            dma((3,)),
+            dma((3,)),
+        ],
+    )(blended, deviation, attended)
+    return blended[None], deviation.T[None], attended[None]
 
 
 def solution(mesh):

time: 122 us -> 105 us (0.86)
  the two profiles are of different devices: /device:TPU:8 before, /device:TPU:1 now
where the time goes in v3:
time: 105 us
  Pallas kernels  103 us (98%)
  other arithmetic  1.4 us (1%)
    pallas_call x1, Pallas kernels, body(): pl.pallas_call(kernel, out_shape=(jax.ShapeDtypeStruct((TOK, KVW), BF16),...  99.9 us
    pallas_call x1, Pallas kernels, body(): pl.pallas_call(hand_on, out_shape=(jax.ShapeDtypeStruct((TOK, KVW), BF16)...  2.93 us

profile of v3, /device:TPU:1, one launch (start us, length us, event | category | flops | bytes accessed | tf_op | source)
XLA Modules:
  0.0 105.0 jit_solution(15969596871355801662)
XLA Ops:
  0.7 0.8 subtract_reduce_fusion
  1.4 0.1 sub.22
  1.5 0.6 pad_convert_fusion.pos
  2.1 99.9 %shard_map.85 = (bf16[896,1024]{1,0:T(8,128)(2,1)}, f32[4,112]{1,0:T(4,128)}, bf16[112,2048]{1,0:T(8,128)(2,1)}) custom-call(s32[16,16]{1,0:T(8,128)} %bitcast.12, s32[16,16]{1,0:T(8,128)} %slot.1, f32[8,128]{1,0:T(8,128)} %pad_convert_fusion.pos, bf16[9,56,1024]{2,1,0:T(8,128)(2,1)} %bitcast.9, bf16[112,2048]{1,0:T(8,128)(2,1)} %bitcast.10, ...), custom_call_target="tpu_custom_call" | custom-call | tf_op jit(solution)/shard_map/pallas_call | solution.py:448
  102.1 2.9 %shard_map.86 = (bf16[896,1024]{1,0:T(8,128)(2,1)}, f32[4,112]{1,0:T(4,128)}, bf16[112,2048]{1,0:T(8,128)(2,1)}) custom-call(bf16[896,1024]{1,0:T(8,128)(2,1)} %get-tuple-element.9.a_in, f32[4,112]{1,0:T(4,128)} %get-tuple-element.10.b_in, bf16[112,2048]{1,0:T(8,128)(2,1)} %get-tuple-element.11.c_in), custom_call_target="tpu_custom_call" | custom-call | tf_op jit(solution)/shard_map/pallas_call | solution.py:489
  (2 shorter events, 0.0 us)
